TPU v7x, 256 devices: a whole 4x4x8 slice. The times are simulated.
256 devices in a mesh: dp: 32 (over x, z), tensor: 8 (over y, core).
Axes of the slice: x: 4, y: 4, z: 8, core: 2. Of those that a mesh axis runs over, the one named last changes fastest.
Arguments:
- context: bfloat16 [2, 32768, 3072], P(None, 'dp', 'tensor'), may hold values from -6 to 6
- out_grad: bfloat16 [2, 32768, 3072], P(None, ('dp', 'tensor')), may hold values from -0.1875 to 0.1875
- error_in: bfloat16 [2, 98304, 3072], P(None, 'dp', 'tensor'), may hold values from -6 to 6
- right_init: float32 [2, 64, 3072], P(None, None, 'tensor'), may hold values from -6 to 6
Outputs:
- summed_update: bfloat16 [2, 3072, 3072], P(None, 'dp', 'tensor')
- error_out: bfloat16 [2, 98304, 3072], P(None, 'dp', 'tensor')
All inputs are finite; a program needn't handle non-finite values.
Results may differ from a plain program's by a relative error of at most 0.015.
Values may be sent and summed in bfloat16 or wider, within the bound.
No kernel may reach another device: no remote copies, remote signals or barrier semaphores. Data moves between devices by JAX's collectives and lax.ppermute only.
A program may use at most 128 MiB of HBM per device.

v0:
```python
import jax
import jax.numpy as jnp
from jax import lax
from jax.sharding import Mesh
from jax.sharding import PartitionSpec as P

TENSOR = ("tensor_0", "tensor_1")
DP_TENSOR = ("dp_0", "dp_1", "tensor_0", "tensor_1")
DP = ("dp_0", "dp_1")


def cut_along(x, dim, devices):
    dims = x.shape
    parts = x.reshape(*dims[:dim], devices, dims[dim] // devices, *dims[dim + 1 :])
    return jnp.moveaxis(parts, dim, 0)


def sent_and_summed(x, axis, dim):
    devices = lax.axis_size(axis)
    parts = lax.all_to_all(cut_along(x, dim, devices), axis, 0, 0, tiled=True)
    return jnp.sum(parts, axis=0)


def sum_in_two_steps(x, axes, dim):
    far, near = axes
    own = sent_and_summed(cut_along(x, dim, lax.axis_size(far)), near, dim + 1)
    return jnp.sum(lax.all_to_all(own, far, 0, 0, tiled=True), axis=0)


def filled_up(lines, devices):
    spare = -lines.shape[0] % devices
    if not spare:
        return lines
    return jnp.concatenate([lines, jnp.zeros((spare, *lines.shape[1:]), lines.dtype)])


def copy_for_each(x, axis):
    devices = lax.axis_size(axis)
    return lax.all_to_all(jnp.broadcast_to(x[None], (devices, *x.shape)), axis, 0, 0, tiled=True)


def joined_along(parts, dim):
    dims = list(parts.shape[1:])
    dims[dim] *= parts.shape[0]
    return jnp.moveaxis(parts, 0, dim).reshape(dims)


def gathered_by_axis(x, axes, dim):
    far, near = axes
    initial = copy_for_each(x, far)
    parts = jnp.swapaxes(copy_for_each(initial, near), 0, 1)
    return joined_along(parts.reshape(-1, *x.shape), dim)


def nested_sum(x, axes):
    lines = x.reshape(-1)
    own = sum_in_two_steps(
        filled_up(lines, lax.axis_size(axes[0]) * lax.axis_size(axes[1])), axes, 0
    )
    whole = gathered_by_axis(own, axes, 0)
    return whole[: len(lines)].reshape(x.shape)


def gathered_copies(x, axis, dim):
    return joined_along(copy_for_each(x, axis), dim)


def summed_on_arrival(x, axis, dim):
    parts = cut_along(x, dim, lax.axis_size(axis))
    arrived = lax.all_to_all(parts, axis, split_axis=0, concat_axis=0, tiled=True)
    return arrived.astype(jnp.float32).sum(axis=0)


def nested_sum_2(x, axes):
    lines = x.reshape(-1, x.shape[-1])
    padded = filled_up(lines, lax.axis_size(axes))
    whole = gathered_copies(summed_on_arrival(padded, axes, 0).astype(jnp.bfloat16), axes, 0)
    return lax.slice_in_dim(whole, 0, len(lines)).reshape(x.shape).astype(jnp.float32)


def solve_rows(gram_matrix, left_factor):
    ridge_term = 1e-06 * jnp.mean(jnp.diagonal(gram_matrix, axis1=1, axis2=2), axis=1)
    eye_matrix = jnp.eye(gram_matrix.shape[1], dtype=gram_matrix.dtype)
    gram_matrix = gram_matrix + ridge_term[:, None, None] * eye_matrix
    factor_low = jnp.linalg.cholesky(gram_matrix)

    def one_solve(low_part, rhs_part):
        return jax.scipy.linalg.solve_triangular(low_part, rhs_part, lower=True)

    return jax.vmap(one_solve)(factor_low, left_factor)


def gram_of(left_factor):
    return jnp.einsum("lrd,lsd->lrs", left_factor, left_factor, precision=lax.Precision.HIGHEST)


def compress(context, out_grad, error_in, right_init):
    out_width = out_grad.shape[2]
    moment = jnp.einsum(
        "ltd,lte->lde",
        lax.all_gather(out_grad, TENSOR, axis=1, tiled=True),
        context,
        preferred_element_type=jnp.float32,
    )
    moment = moment + error_in.astype(jnp.float32)
    left_factor = jnp.einsum("lre,lde->lrd", right_init, moment, precision=lax.Precision.HIGHEST)
    left_factor = nested_sum(left_factor, (("dp_0", "dp_1"), ("tensor_0", "tensor_1")))
    ortho_basis = solve_rows(gram_of(left_factor), left_factor)
    right_terms = jnp.einsum("lrd,lde->lre", ortho_basis, moment, precision=lax.Precision.HIGHEST)
    right_factor = nested_sum_2(right_terms.astype(jnp.bfloat16), DP)
    replicas = lax.axis_size(DP)
    row_share = out_width // replicas
    own_basis = lax.dynamic_slice_in_dim(ortho_basis, lax.axis_index(DP) * row_share, row_share, 2)
    summed = jnp.einsum("lrd,lre->lde", own_basis, right_factor, precision=lax.Precision.HIGHEST)
    mean_part = jnp.einsum(
        "lrd,lre->lde", ortho_basis, right_factor / replicas, precision=lax.Precision.HIGHEST
    )
    new_error = (moment - mean_part).astype(jnp.bfloat16)
    return (summed.astype(jnp.bfloat16), new_error)


def body(context, out_grad, error_in, right_init):
    return compress(context, out_grad, error_in, right_init)


def solution(mesh):
    finer = Mesh(mesh.devices.reshape(4, 8, 4, 2), ("dp_0", "dp_1", "tensor_0", "tensor_1"))
    return jax.shard_map(
        body,
        mesh=finer,
        in_specs=(
            P(None, DP, TENSOR),
            P(None, DP_TENSOR, None),
            P(None, DP, TENSOR),
            P(None, None, TENSOR),
        ),
        out_specs=(P(None, DP, TENSOR), P(None, DP, TENSOR)),
        check_vma=False,
    )
```

profile of v0, /device:TPU:2, one launch (start us, length us, event | category | flops | bytes accessed | tf_op | source)
XLA Modules:
  0.0 293.3 jit_solution(1838412830930112913)
XLA Ops:
  7.2 0.0 copy-start
  7.2 0.0 all-gather.2.cloned.1.call-start
  7.2 2.7 copy.16
  9.9 0.0 all-gather.2.cloned.1.call-update
  9.9 0.0 copy-start.3
  9.9 77.6 %all-gather.2.cloned.1.call-done = bf16[2,1024,3072]{1,2,0:T(8,128)(2,1)} async-done(((bf16[2,128,3072]{1,2,0:T(8,128)(2,1)}), bf16[2,1024,3072]{1,2,0:T(8,128)(2,1)}) %all-gather.2.cloned.1.call-update) | async-done | bytes 12582928 | tf_op jit(solution)/shard_map/all_gather | solution.py:101
  87.5 0.0 copy-done
  87.5 10.4 %convert_add_fusion = f32[2,3072,384]{2,1,0:T(8,128)S(1)} fusion(bf16[2,3072,384]{2,1,0:T(8,128)(2,1)} %param.6, bf16[2,1024,3072]{1,2,0:T(8,128)(2,1)} %all-gather.2.cloned.1.call-done, bf16[2,1024,384]{2,1,0:T(8,128)(2,1)S(1)} %copy-done), kind=kOutput, calls=%fused_computation.2 | convolution fusion | flops 4836556800 | bytes 28311552 | tf_op jit(solution)/shard_map/ltd,lte->lde/dot_general | solution.py:99
  97.9 0.0 copy-start.1
  97.9 3.6 %copy-done.1 = f32[2,3072,384]{2,1,0:T(8,128)} copy-done((f32[2,3072,384]{2,1,0:T(8,128)}, f32[2,3072,384]{2,1,0:T(8,128)S(1)}, u32[]{:S(2)}) %copy-start.1) | copy-done | bytes 9437208
  101.6 0.0 copy-done.3
  101.6 10.7 %convolution_bitcast_fusion = f32[2,64,3072]{2,1,0:T(8,128)} fusion(f32[2,3072,384]{2,1,0:T(8,128)S(1)} %convert_add_fusion, f32[2,64,384]{2,1,0:T(8,128)S(1)} %copy-done.3), kind=kOutput, calls=%fused_computation.3 | convolution fusion | flops 1811939328 | bytes 11206656 | tf_op jit(solution)/shard_map/lre,lde->lrd/dot_general | solution.py:106
  112.3 1.7 reshape_reshape_reshape.6
  114.0 0.9 copy.26
  114.9 25.4 %all_to_all.35 = f32[8,32,1536]{2,1,0:T(8,128)S(1)} all-to-all(f32[8,32,1536]{2,1,0:T(8,128)S(1)} %bitcast.34), channel_id=1, replica_groups=mesh['dp_0'=4,'dp_1'=8,'tensor_0'=4,'tensor_1'=2] {'tensor_0','tensor_1'}, dimensions={0} | all-to-all | bytes 3145728 | tf_op jit(solution)/shard_map/all_to_all | solution.py:20
  140.3 0.1 reduce_sum.39
  140.4 0.1 all_to_all.23
  140.5 19.7 %all_to_all.36 = f32[32,1,1536]{2,1,0:T(1,128)S(1)} all-to-all(f32[32,1,1536]{2,1,0:T(1,128)S(1)} %all_to_all.23), channel_id=1, replica_groups=mesh['dp_0'=4,'dp_1'=8,'tensor_0'=4,'tensor_1'=2] {'dp_0','dp_1'}, dimensions={0} | all-to-all | bytes 393216 | tf_op jit(solution)/shard_map/all_to_all | solution.py:27
  160.2 0.1 reduce_sum.40
  160.4 0.1 broadcast_in_dim.14
  160.5 14.6 %all_to_all.37 = f32[32,1,1536]{2,1,0:T(1,128)S(1)} all-to-all(f32[32,1,1536]{2,1,0:T(1,128)S(1)} %broadcast_in_dim.14), channel_id=1, replica_groups=mesh['dp_0'=4,'dp_1'=8,'tensor_0'=4,'tensor_1'=2] {'dp_0','dp_1'}, dimensions={0} | all-to-all | bytes 393216 | tf_op jit(solution)/shard_map/all_to_all | solution.py:39
  175.1 1.3 broadcast_in_dim.18
  176.4 3.6 %all-to-all-start.3 = ((f32[8,32,1536]{2,1,0:T(8,128)}), f32[8,32,1536]{2,1,0:T(8,128)S(1)}, u32[]{:S(2)}, u32[]{:S(2)}) async-start(f32[8,32,1536]{2,1,0:T(8,128)} %broadcast_in_dim.18), calls=%async_computation.3 | async-start | bytes 3145728 | tf_op jit(solution)/shard_map/all_to_all | solution.py:39
  180.1 21.4 %all-to-all-done.3 = f32[8,32,1536]{2,1,0:T(8,128)S(1)} async-done(((f32[8,32,1536]{2,1,0:T(8,128)}), f32[8,32,1536]{2,1,0:T(8,128)S(1)}, u32[]{:S(2)}, u32[]{:S(2)}) %all-to-all-start.3) | async-done | bytes 1572896 | tf_op jit(solution)/shard_map/all_to_all | solution.py:39
  201.5 2.1 copy.18
  203.5 1.8 reshape_reshape_reshape.7
  205.3 1.6 fusion.12
  206.9 2.0 copy.19
  208.9 0.1 copy.20
  209.0 1.6 gather_fusion
  210.7 0.1 fusion.6
  210.7 11.7 %custom-call.8 = f32[2,64,64]{2,1,0:T(8,128)S(1)} custom-call(f32[2,64,64]{2,1,0:T(8,128)S(1)} %fusion.6), custom_call_target="Cholesky" | custom-call | tf_op jit(solution)/shard_map/jit(cholesky)/cholesky | solution.py:85
  222.5 0.1 compare_reduce_fusion
  222.6 0.1 select_bitcast_fusion
  222.7 9.8 %custom-call.9 = f32[2,1,64,64]{2,3,1,0:T(8,128)S(1)} custom-call(f32[2,1,64,64]{3,2,1,0:T(8,128)S(1)} %select_bitcast_fusion), custom_call_target="InvertDiagBlocksLowerTriangular" | custom-call | tf_op jit(solution)/shard_map/vmap(jit(_solve_triangular))/triangular_solve | solution.py:88
  232.5 1.5 fusion.3
  234.1 0.0 copy-start.2
  234.1 1.2 copy-done.2
  235.2 8.2 %convolution_convert_fusion.1 = bf16[2,64,384]{2,1,0:T(8,128)(2,1)S(1)} fusion(f32[2,64,3072]{2,1,0:T(8,128)S(1)} %fusion.3, f32[2,3072,384]{2,1,0:T(8,128)} %copy-done.1), kind=kOutput, calls=%fused_computation.6 | convolution fusion | flops 1811988480 | bytes 11108352 | tf_op jit(solution)/shard_map/lrd,lde->lre/dot_general | solution.py:109
  243.4 14.0 %all_to_all.38 = bf16[32,4,384]{2,1,0:T(4,128)(2,1)S(1)} all-to-all(bf16[32,4,384]{2,1,0:T(4,128)(2,1)S(1)} %reshape_reshape.6), channel_id=1, replica_groups=mesh['dp_0'=4,'dp_1'=8,'tensor_0'=4,'tensor_1'=2] {'dp_0','dp_1'}, dimensions={0} | all-to-all | bytes 196608 | tf_op jit(solution)/shard_map/all_to_all | solution.py:70
  257.5 0.1 reduce_sum.42
  257.5 0.7 broadcast_in_dim.19
  258.2 5.0 %all-to-all-start.5 = ((bf16[32,4,384]{2,1,0:T(4,128)(2,1)}), bf16[32,4,384]{2,1,0:T(4,128)(2,1)S(1)}, u32[]{:S(2)}, u32[]{:S(2)}) async-start(bf16[32,4,384]{2,1,0:T(4,128)(2,1)} %broadcast_in_dim.19), calls=%async_computation.5 | async-start | bytes 196608 | tf_op jit(solution)/shard_map/all_to_all | solution.py:39
  263.2 9.1 %all-to-all-done.5 = bf16[32,4,384]{2,1,0:T(4,128)(2,1)S(1)} async-done(((bf16[32,4,384]{2,1,0:T(4,128)(2,1)}), bf16[32,4,384]{2,1,0:T(4,128)(2,1)S(1)}, u32[]{:S(2)}, u32[]{:S(2)}) %all-to-all-start.5) | async-done | bytes 98336 | tf_op jit(solution)/shard_map/all_to_all | solution.py:39
  272.3 12.1 %subtract_convert_fusion = bf16[2,3072,384]{2,1,0:T(8,128)(2,1)} fusion(f32[2,3072,384]{2,1,0:T(8,128)} %copy-done.1, f32[2,64,3072]{2,1,0:T(8,128)} %copy-done.2, bf16[2,64,384]{2,1,0:T(8,128)(2,1)S(1)} %reshape_reshape.7), kind=kOutput, calls=%fused_computation.1 | convolution fusion | flops 1816756224 | bytes 15826944 | tf_op jit(solution)/shard_map/lrd,lre->lde/dot_general | solution.py:115
  284.5 2.0 convolution_convert_fusion
  (10 shorter events, 0.2 us)
Async XLA Ops:
  7.2 80.4 %copy-start = (bf16[2,1024,384]{2,1,0:T(8,128)(2,1)S(1)}, bf16[2,1024,384]{2,1,0:T(8,128)(2,1)}, u32[]{:S(2)}) copy-start(bf16[2,1024,384]{2,1,0:T(8,128)(2,1)} %param.4) | copy-start | bytes 4718596
  7.2 80.3 %all-gather.2.cloned.1.call-start = ((), (), s32[]{:S(2)}) async-start(), calls=%async_computation.6 | async-start | bytes 14155776 | tf_op jit(solution)/shard_map/all_gather | solution.py:101
  9.9 91.6 %copy-start.3 = (f32[2,64,384]{2,1,0:T(8,128)S(1)}, f32[2,64,384]{2,1,0:T(8,128)}, u32[]{:S(2)}) copy-start(f32[2,64,384]{2,1,0:T(8,128)} %param.7) | copy-start | bytes 589828
  97.9 3.6 %copy-start.1 = (f32[2,3072,384]{2,1,0:T(8,128)}, f32[2,3072,384]{2,1,0:T(8,128)S(1)}, u32[]{:S(2)}) copy-start(f32[2,3072,384]{2,1,0:T(8,128)S(1)} %convert_add_fusion) | copy-start | bytes 28311556
  176.4 25.1 %all-to-all-start.3 = ((f32[8,32,1536]{2,1,0:T(8,128)}), f32[8,32,1536]{2,1,0:T(8,128)S(1)}, u32[]{:S(2)}, u32[]{:S(2)}) async-start(f32[8,32,1536]{2,1,0:T(8,128)} %broadcast_in_dim.18), calls=%async_computation.3 | async-start | bytes 3145728 | tf_op jit(solution)/shard_map/all_to_all | solution.py:39
  234.1 1.2 copy-start.2
  258.2 14.1 %all-to-all-start.5 = ((bf16[32,4,384]{2,1,0:T(4,128)(2,1)}), bf16[32,4,384]{2,1,0:T(4,128)(2,1)S(1)}, u32[]{:S(2)}, u32[]{:S(2)}) async-start(bf16[32,4,384]{2,1,0:T(4,128)(2,1)} %broadcast_in_dim.19), calls=%async_computation.5 | async-start | bytes 196608 | tf_op jit(solution)/shard_map/all_to_all | solution.py:39
Sparse Core Ops, SparseCore 0:
  10.4 77.0 all-gather.1
where the time goes:
time: 294 us; the launch traced here: 293 us
  waiting for transfers between devices  108 us (37%)
  blocking collectives  73.7 us (25%)
  matrix products  46.4 us (16%)
  other arithmetic  22.2 us (8%)
  local copies, waits for them, and re-layouts  20 us (7%)
  between operations  14.2 us (5%)
  starting transfers between devices  8.59 us (3%)
    all_gather x1, waiting for transfers between devices, compress(): lax.all_gather(out_grad, TENSOR, axis=1, tiled=True)  77.6 us
    all_to_all x2, waiting for transfers between devices, copy_for_each(): lax.all_to_all(jnp.broadcast_to(x[None], (devices, *x.shape)), axis, 0, 0...  30.5 us
    all_to_all x1, blocking collectives, sent_and_summed(): parts = lax.all_to_all(cut_along(x, dim, devices), axis, 0, 0, tiled=True)  25.4 us
    all_to_all x1, blocking collectives, sum_in_two_steps(): return jnp.sum(lax.all_to_all(own, far, 0, 0, tiled=True), axis=0)  19.7 us
    all_to_all x1, blocking collectives, copy_for_each(): lax.all_to_all(jnp.broadcast_to(x[None], (devices, *x.shape)), axis, 0, 0...  14.6 us
    all_to_all x1, blocking collectives, summed_on_arrival(): lax.all_to_all(parts, axis, split_axis=0, concat_axis=0, tiled=True)  14 us
    dot_general x1, matrix products, compress(): jnp.einsum('lrd,lre->lde', ortho_basis, right_factor / replicas, precisio...  12.1 us
    another operation x4, other arithmetic, solve_rows(): factor_low = jnp.linalg.cholesky(gram_matrix)  11.9 us
  transfers between devices with their start and end apart: 3, of which 3 were waited for; matrix products, arithmetic and copies ran while one was open for 0% of the time, Pallas kernels for 0%

commit v1 on v0

--- a/solution.py
+++ b/solution.py
@@ -98,7 +98,9 @@
     out_width = out_grad.shape[2]
     moment = jnp.einsum(
         "ltd,lte->lde",
-        lax.all_gather(out_grad, TENSOR, axis=1, tiled=True),
+        jnp.concatenate(
+            lax.all_to_all(jnp.stack([out_grad] * lax.axis_size(TENSOR)), TENSOR, 0, 0), axis=1
+        ),
         context,
         preferred_element_type=jnp.float32,
     )

time: 294 us -> 349 us (1.19)
  blocking collectives: 73.7 us -> 221 us
  waiting for transfers between devices: 108 us -> 30.3 us
  between operations: 14.2 us -> 0.82 us
    all_to_all x0 -> x1, blocking collectives: none -> 146 us  [compress(): lax.all_to_all(jnp.stack([out_grad] * lax.axis_size(TENSOR)), TENSOR, 0, 0)]
    all_gather x1 -> x0, waiting for transfers between devices: 77.6 us -> none  [compress(): lax.all_gather(out_grad, TENSOR, axis=1, tiled=True)]
    another operation x0 -> x1, local copies, waits for them, and re-layouts: none -> 7 us  [compress(): jnp.stack([out_grad] * lax.axis_size(TENSOR))]
  transfers between devices with their start and end apart: 3 -> 2, of which waited for: 3 -> 2; matrix products, arithmetic and copies ran while one was open for 0% -> 0% of each run, Pallas kernels for 0% -> 0%
where the time goes in v1:
time: 349 us
  blocking collectives  221 us (63%)
  matrix products  44.4 us (13%)
  waiting for transfers between devices  30.3 us (9%)
  other arithmetic  22.2 us (6%)
  local copies, waits for them, and re-layouts  21.2 us (6%)
  starting transfers between devices  8.78 us (3%)
    all_to_all x1, blocking collectives, compress(): lax.all_to_all(jnp.stack([out_grad] * lax.axis_size(TENSOR)), TENSOR, 0, 0)  146 us
    all_to_all x2, waiting for transfers between devices, copy_for_each(): lax.all_to_all(jnp.broadcast_to(x[None], (devices, *x.shape)), axis, 0, 0...  30.3 us
    all_to_all x1, blocking collectives, sent_and_summed(): parts = lax.all_to_all(cut_along(x, dim, devices), axis, 0, 0, tiled=True)  25 us
    all_to_all x1, blocking collectives, sum_in_two_steps(): return jnp.sum(lax.all_to_all(own, far, 0, 0, tiled=True), axis=0)  21.2 us
    all_to_all x1, blocking collectives, copy_for_each(): lax.all_to_all(jnp.broadcast_to(x[None], (devices, *x.shape)), axis, 0, 0...  14.6 us
    all_to_all x1, blocking collectives, summed_on_arrival(): lax.all_to_all(parts, axis, split_axis=0, concat_axis=0, tiled=True)  14 us
    another operation x4, other arithmetic, solve_rows(): factor_low = jnp.linalg.cholesky(gram_matrix)  11.9 us
    dot_general x1, matrix products, compress(): jnp.einsum('lrd,lre->lde', ortho_basis, right_factor / replicas, precisio...  11.6 us
  transfers between devices with their start and end apart: 2, of which 2 were waited for; matrix products, arithmetic and copies ran while one was open for 0% of the time, Pallas kernels for 0%

profile of v1, /device:TPU:2, one launch (start us, length us, event | category | flops | bytes accessed | tf_op | source)
XLA Modules:
  0.0 348.9 jit_solution(12536229819782741604)
XLA Ops:
  0.6 0.0 copy-start
  0.6 2.0 copy.17
  2.7 7.0 %stack.2 = bf16[8,2,128,3072]{2,3,1,0:T(8,128)(2,1)} broadcast(bf16[2,128,3072]{1,2,0:T(8,128)(2,1)S(1)} %copy.17), dimensions={1,2,3} | broadcast | bytes 14155776 | tf_op jit(solution)/shard_map/stack | solution.py:102
  9.7 146.3 %all_to_all.40 = bf16[8,2,128,3072]{2,3,1,0:T(8,128)(2,1)} all-to-all(bf16[8,2,128,3072]{2,3,1,0:T(8,128)(2,1)} %stack.2), channel_id=1, replica_groups=mesh['dp_0'=4,'dp_1'=8,'tensor_0'=4,'tensor_1'=2] {'tensor_0','tensor_1'}, dimensions={0} | all-to-all | bytes 25165824 | tf_op jit(solution)/shard_map/all_to_all | solution.py:102
  156.0 0.0 copy-done
  156.0 0.0 copy-start.3
  156.0 11.0 %convert_add_fusion = f32[2,3072,384]{2,1,0:T(8,128)S(1)} fusion(bf16[2,3072,384]{2,1,0:T(8,128)(2,1)} %param.6, bf16[2,1024,384]{2,1,0:T(8,128)(2,1)S(1)} %copy-done, bf16[8,2,128,3072]{2,3,1,0:T(8,128)(2,1)} %all_to_all.40), kind=kOutput, calls=%fused_computation.5 | convolution fusion | flops 4836556800 | bytes 28311552 | tf_op jit(solution)/shard_map/ltd,lte->lde/dot_general | solution.py:99
  167.0 0.0 copy-start.2
  167.0 3.6 %copy-done.2 = f32[2,3072,384]{2,1,0:T(8,128)} copy-done((f32[2,3072,384]{2,1,0:T(8,128)}, f32[2,3072,384]{2,1,0:T(8,128)S(1)}, u32[]{:S(2)}) %copy-start.2) | copy-done | bytes 9437208
  170.6 0.0 copy-done.3
  170.6 9.5 %convolution_bitcast_fusion = f32[2,64,3072]{2,1,0:T(8,128)S(1)} fusion(f32[2,3072,384]{2,1,0:T(8,128)S(1)} %convert_add_fusion, f32[2,64,384]{2,1,0:T(8,128)S(1)} %copy-done.3), kind=kOutput, calls=%fused_computation.6 | convolution fusion | flops 1811939328 | bytes 11206656 | tf_op jit(solution)/shard_map/lre,lde->lrd/dot_general | solution.py:108
  180.1 0.2 reshape_reshape_reshape.6
  180.4 0.9 copy.35
  181.3 25.0 %all_to_all.41 = f32[8,32,1536]{2,1,0:T(8,128)S(1)} all-to-all(f32[8,32,1536]{2,1,0:T(8,128)S(1)} %bitcast.43), channel_id=1, replica_groups=mesh['dp_0'=4,'dp_1'=8,'tensor_0'=4,'tensor_1'=2] {'tensor_0','tensor_1'}, dimensions={0} | all-to-all | bytes 3145728 | tf_op jit(solution)/shard_map/all_to_all | solution.py:20
  206.3 0.1 reduce_sum.39
  206.4 0.1 all_to_all.27
  206.6 21.2 %all_to_all.42 = f32[32,1,1536]{2,1,0:T(1,128)S(1)} all-to-all(f32[32,1,1536]{2,1,0:T(1,128)S(1)} %all_to_all.27), channel_id=1, replica_groups=mesh['dp_0'=4,'dp_1'=8,'tensor_0'=4,'tensor_1'=2] {'dp_0','dp_1'}, dimensions={0} | all-to-all | bytes 393216 | tf_op jit(solution)/shard_map/all_to_all | solution.py:27
  227.7 0.1 reduce_sum.40
  227.9 0.1 broadcast_in_dim.14
  228.0 14.6 %all_to_all.43 = f32[32,1,1536]{2,1,0:T(1,128)S(1)} all-to-all(f32[32,1,1536]{2,1,0:T(1,128)S(1)} %broadcast_in_dim.14), channel_id=1, replica_groups=mesh['dp_0'=4,'dp_1'=8,'tensor_0'=4,'tensor_1'=2] {'dp_0','dp_1'}, dimensions={0} | all-to-all | bytes 393216 | tf_op jit(solution)/shard_map/all_to_all | solution.py:39
  242.6 1.3 broadcast_in_dim.18
  243.9 3.8 %all-to-all-start.4 = ((f32[8,32,1536]{2,1,0:T(8,128)}), f32[8,32,1536]{2,1,0:T(8,128)S(1)}, u32[]{:S(2)}, u32[]{:S(2)}) async-start(f32[8,32,1536]{2,1,0:T(8,128)} %broadcast_in_dim.18), calls=%async_computation.4 | async-start | bytes 3145728 | tf_op jit(solution)/shard_map/all_to_all | solution.py:39
  247.8 21.2 %all-to-all-done.4 = f32[8,32,1536]{2,1,0:T(8,128)S(1)} async-done(((f32[8,32,1536]{2,1,0:T(8,128)}), f32[8,32,1536]{2,1,0:T(8,128)S(1)}, u32[]{:S(2)}, u32[]{:S(2)}) %all-to-all-start.4) | async-done | bytes 1572896 | tf_op jit(solution)/shard_map/all_to_all | solution.py:39
  269.0 0.9 copy.20
  269.9 0.5 reshape_reshape_reshape.7
  270.4 1.6 fusion.17
  272.0 2.0 copy.21
  274.0 0.1 copy.22
  274.1 1.6 gather_fusion
  275.7 0.1 fusion.11
  275.8 11.7 %custom-call.8 = f32[2,64,64]{2,1,0:T(8,128)S(1)} custom-call(f32[2,64,64]{2,1,0:T(8,128)S(1)} %fusion.11), custom_call_target="Cholesky" | custom-call | tf_op jit(solution)/shard_map/jit(cholesky)/cholesky | solution.py:85
  287.6 0.1 compare_reduce_fusion
  287.7 0.1 select_bitcast_fusion
  287.8 9.8 %custom-call.9 = f32[2,1,64,64]{2,3,1,0:T(8,128)S(1)} custom-call(f32[2,1,64,64]{3,2,1,0:T(8,128)S(1)} %select_bitcast_fusion), custom_call_target="InvertDiagBlocksLowerTriangular" | custom-call | tf_op jit(solution)/shard_map/vmap(jit(_solve_triangular))/triangular_solve | solution.py:88
  297.6 1.5 fusion.8
  299.1 8.1 %convolution_convert_fusion.1 = bf16[2,64,384]{2,1,0:T(8,128)(2,1)S(1)} fusion(f32[2,64,3072]{2,1,0:T(8,128)S(1)} %fusion.8, f32[2,3072,384]{2,1,0:T(8,128)} %copy-done.2), kind=kOutput, calls=%fused_computation.9 | convolution fusion | flops 1811988480 | bytes 11108352 | tf_op jit(solution)/shard_map/lrd,lde->lre/dot_general | solution.py:111
  307.3 14.0 %all_to_all.44 = bf16[32,4,384]{2,1,0:T(4,128)(2,1)S(1)} all-to-all(bf16[32,4,384]{2,1,0:T(4,128)(2,1)S(1)} %reshape_reshape.6), channel_id=1, replica_groups=mesh['dp_0'=4,'dp_1'=8,'tensor_0'=4,'tensor_1'=2] {'dp_0','dp_1'}, dimensions={0} | all-to-all | bytes 196608 | tf_op jit(solution)/shard_map/all_to_all | solution.py:70
  321.4 0.1 reduce_sum.42
  321.4 0.7 broadcast_in_dim.19
  322.1 5.0 %all-to-all-start.6 = ((bf16[32,4,384]{2,1,0:T(4,128)(2,1)}), bf16[32,4,384]{2,1,0:T(4,128)(2,1)S(1)}, u32[]{:S(2)}, u32[]{:S(2)}) async-start(bf16[32,4,384]{2,1,0:T(4,128)(2,1)} %broadcast_in_dim.19), calls=%async_computation.6 | async-start | bytes 196608 | tf_op jit(solution)/shard_map/all_to_all | solution.py:39
  327.1 9.1 %all-to-all-done.6 = bf16[32,4,384]{2,1,0:T(4,128)(2,1)S(1)} async-done(((bf16[32,4,384]{2,1,0:T(4,128)(2,1)}), bf16[32,4,384]{2,1,0:T(4,128)(2,1)S(1)}, u32[]{:S(2)}, u32[]{:S(2)}) %all-to-all-start.6) | async-done | bytes 98336 | tf_op jit(solution)/shard_map/all_to_all | solution.py:39
  336.2 0.0 copy-start.1
  336.2 11.6 %subtract_convert_fusion = bf16[2,3072,384]{2,1,0:T(8,128)(2,1)} fusion(f32[2,3072,384]{2,1,0:T(8,128)} %copy-done.2, f32[2,64,3072]{2,1,0:T(8,128)S(1)} %fusion.8, bf16[2,64,384]{2,1,0:T(8,128)(2,1)S(1)} %reshape_reshape.7), kind=kOutput, calls=%fused_computation.4 | convolution fusion | flops 1816756224 | bytes 15826944 | tf_op jit(solution)/shard_map/lrd,lre->lde/dot_general | solution.py:117
  347.8 1.1 convolution_convert_fusion
  348.9 0.0 copy-done.1
  (10 shorter events, 0.2 us)
Async XLA Ops:
  0.6 155.3 %copy-start = (bf16[2,1024,384]{2,1,0:T(8,128)(2,1)S(1)}, bf16[2,1024,384]{2,1,0:T(8,128)(2,1)}, u32[]{:S(2)}) copy-start(bf16[2,1024,384]{2,1,0:T(8,128)(2,1)} %param.4) | copy-start | bytes 4718596
  156.0 14.6 %copy-start.3 = (f32[2,64,384]{2,1,0:T(8,128)S(1)}, f32[2,64,384]{2,1,0:T(8,128)}, u32[]{:S(2)}) copy-start(f32[2,64,384]{2,1,0:T(8,128)} %param.7) | copy-start | bytes 589828
  167.0 3.6 %copy-start.2 = (f32[2,3072,384]{2,1,0:T(8,128)}, f32[2,3072,384]{2,1,0:T(8,128)S(1)}, u32[]{:S(2)}) copy-start(f32[2,3072,384]{2,1,0:T(8,128)S(1)} %convert_add_fusion) | copy-start | bytes 28311556
  243.9 25.1 %all-to-all-start.4 = ((f32[8,32,1536]{2,1,0:T(8,128)}), f32[8,32,1536]{2,1,0:T(8,128)S(1)}, u32[]{:S(2)}, u32[]{:S(2)}) async-start(f32[8,32,1536]{2,1,0:T(8,128)} %broadcast_in_dim.18), calls=%async_computation.4 | async-start | bytes 3145728 | tf_op jit(solution)/shard_map/all_to_all | solution.py:39
  322.1 14.1 %all-to-all-start.6 = ((bf16[32,4,384]{2,1,0:T(4,128)(2,1)}), bf16[32,4,384]{2,1,0:T(4,128)(2,1)S(1)}, u32[]{:S(2)}, u32[]{:S(2)}) async-start(bf16[32,4,384]{2,1,0:T(4,128)(2,1)} %broadcast_in_dim.19), calls=%async_computation.6 | async-start | bytes 196608 | tf_op jit(solution)/shard_map/all_to_all | solution.py:39
  336.2 12.7 %copy-start.1 = (bf16[2,1024,384]{2,1,0:T(8,128)(2,1)S(1)}, bf16[2,1024,384]{2,1,0:T(8,128)(2,1)}, u32[]{:S(2)}) copy-start(bf16[2,1024,384]{2,1,0:T(8,128)(2,1)} %param.4) | copy-start | bytes 4718596
